TPU v7x, 32 devices: a whole 2x2x4 slice. The times are simulated.
32 devices in a mesh: spatial: 8 (over z, x), filter: 4 (over y, core).
Axes of the slice: x: 2, y: 2, z: 4, core: 2. Of those that a mesh axis runs over, the one named last changes fastest.
Arguments:
- volume_in: bfloat16 [128, 32, 8192], P('filter', 'spatial'), may hold values from -6 to 6
- filters_a: bfloat16 [27, 256, 128], P(None, 'filter'), may hold values from -0.109375 to 0.109375
- bias_a: bfloat16 [256], P('filter'), may hold values from -0.5 to 0.5
- filters_b: bfloat16 [27, 256, 256], P(None, 'filter'), may hold values from -0.078125 to 0.078125
- bias_b: bfloat16 [256], P('filter'), may hold values from -0.5 to 0.5
Outputs:
- volume_out: bfloat16 [256, 8, 512], P('filter', 'spatial')
All inputs are finite; a program needn't handle non-finite values.
Results may differ from a plain program's by a relative error of at most 0.0048.
Values may be sent and summed in bfloat16 or wider, within the bound.
A program may use at most 128 MiB of HBM per device.

v0:
```python
import jax
import jax.numpy as jnp
from jax import lax
from jax.sharding import PartitionSpec as P

ROWS = 64
COLS = 128


def shifted(block, axis, distance):
    devices = range(lax.axis_size(axis))
    route = [(i - distance, i) for i in devices if i - distance in devices]
    return lax.ppermute(block, axis, route)


def local_conv(block, weight, pad_rows, row_count, col_count):
    channels = block.shape[0]
    slices = block.shape[1]
    volume = block.reshape(1, channels, slices, row_count, col_count)
    kernel = weight.reshape(3, 3, 3, weight.shape[1], weight.shape[2])
    return lax.conv_general_dilated(
        volume,
        kernel,
        (2, 2, 2),
        ((0, 0), (pad_rows, pad_rows), (1, 1)),
        dimension_numbers=("NCDHW", "DHWOI", "NCDHW"),
        preferred_element_type=jnp.float32,
    )[0]


def activate(summed, bias_vec):
    summed = summed + bias_vec.astype(jnp.float32)[:, None, None, None]
    return jnp.where(summed > 0, summed, 0.2 * summed).astype(jnp.bfloat16)


def per_device(volume_in, filters_a, bias_a, filters_b, bias_b):
    slices = volume_in.shape[1]
    outputs = filters_a.shape[1]
    beneath = shifted(volume_in[:, -1:], "spatial", 1)
    extended = jnp.concatenate([beneath, volume_in], 1)
    zeros_first = jnp.zeros((outputs, slices // 2, ROWS // 2, COLS // 2), jnp.float32)
    weight_part = filters_a
    summed = zeros_first + local_conv(
        lax.all_gather(extended, "filter", axis=0, tiled=True), weight_part, 1, ROWS, COLS
    )
    hidden = activate(summed, bias_a).reshape(outputs, slices // 2, ROWS // 2 * (COLS // 2))
    beneath_two = shifted(hidden[:, -1:], "spatial", 1)
    extended_two = jnp.concatenate([beneath_two, hidden], 1)
    zeros_second = jnp.zeros((filters_b.shape[1], slices // 4, ROWS // 4, COLS // 4), jnp.float32)
    weight_part = filters_b
    summed_two = zeros_second + local_conv(
        lax.all_gather(extended_two, "filter", axis=0, tiled=True),
        weight_part,
        1,
        ROWS // 2,
        COLS // 2,
    )
    return activate(summed_two, bias_b).reshape(
        filters_b.shape[1], slices // 4, ROWS // 4 * (COLS // 4)
    )


def solution(mesh):
    in_specs = (
        P("filter", "spatial", None),
        P(None, "filter", None),
        P("filter"),
        P(None, "filter", None),
        P("filter"),
    )
    out_specs = P("filter", "spatial", None)
    return jax.shard_map(
        per_device, mesh=mesh, in_specs=in_specs, out_specs=out_specs, check_vma=False
    )
```

profile of v0, /device:TPU:0, one launch (start us, length us, event | category | flops | bytes accessed | tf_op | source)
XLA Modules:
  0.0 223.8 jit_solution(5031182525449573084)
XLA Ops:
  6.5 0.0 copy-start
  6.5 0.0 all-gather.3.cloned.1.call-start
  6.5 2.8 %copy.46 = bf16[32,4,8192]{2,0,1:T(8,128)(2,1)S(1)} copy(bf16[32,4,8192]{2,1,0:T(4,128)(2,1)} %param.5) | data formatting | bytes 4194304 | tf_op args[0]
  9.4 0.0 copy-start.2
  9.4 4.9 %collective-permute-start = (bf16[32,1,8192]{2,0,1:T(8,128)(2,1)S(1)}, bf16[32,1,8192]{2,0,1:T(8,128)(2,1)S(1)}, u32[]{:S(2)}, u32[]{:S(2)}) collective-permute-start(bf16[32,1,8192]{2,0,1:T(8,128)(2,1)S(1)} %slice.12), channel_id=1, source_target_pairs={{0,4},{4,8},{8,12},{12,16},{16,20},{20,24},{24,28},{1,5},{5,9},{9,... | collective-permute-start | bytes 1572872 | tf_op jit(solution)/shard_map/ppermute | solution.py:13
  14.3 11.1 %collective-permute-done = bf16[32,1,8192]{2,0,1:T(8,128)(2,1)S(1)} collective-permute-done((bf16[32,1,8192]{2,0,1:T(8,128)(2,1)S(1)}, bf16[32,1,8192]{2,0,1:T(8,128)(2,1)S(1)}, u32[]{:S(2)}, u32[]{:S(2)}) %collective-permute-start) | collective-permute-done | bytes 524320 | tf_op jit(solution)/shard_map/ppermute | solution.py:13
  25.4 1.8 pad_maximum_fusion
  27.2 0.0 all-gather.3.cloned.1.call-update
  27.2 0.0 all-gather.5.cloned.1.call-start
  27.3 0.0 copy-done.2
  27.3 72.5 %all-gather.3.cloned.1.call-done = bf16[128,5,8192]{2,0,1:T(8,128)(2,1)} async-done(((bf16[32,5,8192]{2,0,1:T(8,128)(2,1)}), bf16[128,5,8192]{2,0,1:T(8,128)(2,1)}) %all-gather.3.cloned.1.call-update) | async-done | bytes 10485776 | tf_op jit(solution)/shard_map/all_gather | solution.py:44
  99.8 14.2 %copy.48 = bf16[128,5,8192]{0,2,1:T(8,128)(2,1)} copy(bf16[128,5,8192]{2,0,1:T(8,128)(2,1)} %all-gather.3.cloned.1.call-done) | data formatting | bytes 20971520 | tf_op jit(solution)/shard_map/all_gather | solution.py:44
  114.0 14.7 %copy.61 = bf16[128,5,64,1,128]{0,2,4,1,3:T(8,128)(2,1)} copy(bf16[128,5,64,1,128]{0,4,2,1,3:T(8,128)(2,1)} %bitcast.31) | data formatting | bytes 20971520
  128.8 6.4 %pad.clone = bf16[128,5,64,1,144]{0,2,4,1,3:T(8,128)(2,1)S(1)} pad(bf16[128,5,64,1,128]{0,2,4,1,3:T(8,128)(2,1)} %copy.61, bf16[]{:T(256)} %constant.1), padding=0_0x0_0x0_0x0_0x1_15 | pad | bytes 22282242 | tf_op jit(solution)/shard_map/reshape | solution.py:19
  135.2 0.0 copy-start.1
  135.2 0.0 copy-start.4
  135.2 8.6 %copy.51 = bf16[128,5,64,1,8,18]{0,4,5,2,1,3:T(8,128)(2,1)S(1)} copy(bf16[128,5,64,1,8,18]{0,2,5,4,1,3:T(8,128)(2,1)S(1)} %bitcast.30) | data formatting | bytes 23592960 | tf_op jit(solution)/shard_map/conv_general_dilated | solution.py:21
  143.9 0.3 slice.13
  144.2 0.0 copy-done.1
  144.2 0.0 copy-done.4
  144.2 10.2 %fusion.12 = f32[2,32,8,9,64]{4,2,3,1,0:T(8,128)} fusion(bf16[3,3,3,64,128]{4,3,2,1,0:T(8,128)(2,1)S(1)} %bitcast.37, bf16[128,5,64,1,7,2]{0,4,5,2,1,3:T(8,128)(2,1)S(1)} %slice.13, bf16[128,5,64,1,8,18]{0,4,5,2,1,3:T(8,128)(2,1)S(1)} %copy.51, pred[8,9]{0,1:T(8,128)(4,1)S(1)} %copy-done.4), kind=kOutput, calls=%fused_computation.15 | convolution fusion | flops 2056814592 | bytes 14565448 | tf_op jit(solution)/shard_map/conv_general_dilated | solution.py:21
  154.5 2.1 copy.52
  156.6 0.2 slice_bitcast_fusion
  156.8 3.1 %copy.53 = f32[1,64,2,32,64]{4,3,1,2,0:T(8,128)} copy(f32[1,64,2,32,64]{1,3,4,2,0:T(8,128)S(1)} %slice_bitcast_fusion) | data formatting | bytes 2097152 | tf_op jit(solution)/shard_map/conv_general_dilated | solution.py:21
  159.8 0.0 copy-start.3
  159.8 2.1 squeeze.6
  161.9 0.2 fusion.18
  162.2 3.4 %collective-permute-start.1 = (bf16[64,1,2048]{2,0,1:T(8,128)(2,1)S(1)}, bf16[64,1,2048]{2,0,1:T(8,128)(2,1)S(1)}, u32[]{:S(2)}, u32[]{:S(2)}) collective-permute-start(bf16[64,1,2048]{2,0,1:T(8,128)(2,1)S(1)} %slice.15), channel_id=1, source_target_pairs={{0,4},{4,8},{8,12},{12,16},{16,20},{20,24},{24,28},{1,5},{5,9},{9,... | collective-permute-start | bytes 786440 | tf_op jit(solution)/shard_map/ppermute | solution.py:13
  165.6 6.0 %collective-permute-done.1 = bf16[64,1,2048]{2,0,1:T(8,128)(2,1)S(1)} collective-permute-done((bf16[64,1,2048]{2,0,1:T(8,128)(2,1)S(1)}, bf16[64,1,2048]{2,0,1:T(8,128)(2,1)S(1)}, u32[]{:S(2)}, u32[]{:S(2)}) %collective-permute-start.1) | collective-permute-done | bytes 262176 | tf_op jit(solution)/shard_map/ppermute | solution.py:13
  171.5 1.0 pad_maximum_fusion.1
  172.5 0.0 all-gather.5.cloned.1.call-update
  172.5 0.0 copy-done.3
  172.6 29.7 %all-gather.5.cloned.1.call-done = bf16[256,3,2048]{2,0,1:T(8,128)(2,1)} async-done(((bf16[64,3,2048]{2,0,1:T(8,128)(2,1)}), bf16[256,3,2048]{2,0,1:T(8,128)(2,1)}) %all-gather.5.cloned.1.call-update) | async-done | bytes 3145744 | tf_op jit(solution)/shard_map/all_gather | solution.py:52
  202.2 4.6 %copy.54 = bf16[256,3,2048]{0,2,1:T(8,128)(2,1)} copy(bf16[256,3,2048]{2,0,1:T(8,128)(2,1)} %all-gather.5.cloned.1.call-done) | data formatting | bytes 6291456 | tf_op jit(solution)/shard_map/all_gather | solution.py:52
  206.9 3.7 %copy.62 = bf16[256,3,32,1,64]{0,2,4,1,3:T(8,128)(2,1)S(1)} copy(bf16[256,3,32,1,64]{0,4,2,1,3:T(8,128)(2,1)} %bitcast.33) | data formatting | bytes 6291456
  210.6 0.4 pad.2.clone
  211.0 0.0 copy-start.5
  211.0 2.3 %copy.57 = bf16[256,3,32,1,8,10]{0,4,5,2,1,3:T(8,128)(2,1)S(1)} copy(bf16[256,3,32,1,8,10]{0,2,5,4,1,3:T(8,128)(2,1)S(1)} %bitcast.32) | data formatting | bytes 7864320 | tf_op jit(solution)/shard_map/conv_general_dilated | solution.py:21
  213.3 0.2 slice.16
  213.5 0.0 copy-done
  213.5 0.0 copy-done.5
  213.5 2.5 %fusion.15 = f32[1,16,8,5,64]{4,2,3,1,0:T(8,128)S(1)} fusion(bf16[3,3,3,64,256]{4,3,2,1,0:T(8,128)(2,1)S(1)} %bitcast.29, bf16[256,3,32,1,7,2]{0,4,5,2,1,3:T(8,128)(2,1)S(1)} %slice.16, bf16[256,3,32,1,8,10]{0,4,5,2,1,3:T(8,128)(2,1)S(1)} %copy.57, pred[8,5]{0,1:T(8,128)(4,1)S(1)} %copy-done.5), kind=kOutput, calls=%fused_computation.16 | convolution fusion | flops 568631296 | bytes 5668904 | tf_op jit(solution)/shard_map/conv_general_dilated | solution.py:21
  216.0 0.1 copy.58
  216.1 0.1 copy.59
  216.1 0.1 copy.60
  216.3 0.7 fusion.19
  (5 shorter events, 0.1 us)
Async XLA Ops:
  6.5 206.9 %copy-start = (bf16[27,64,256]{2,1,0:T(8,128)(2,1)S(1)}, bf16[27,64,256]{2,1,0:T(8,128)(2,1)}, u32[]{:S(2)}) copy-start(bf16[27,64,256]{2,1,0:T(8,128)(2,1)} %param.8) | copy-start | bytes 2654212
  6.5 93.3 %all-gather.3.cloned.1.call-start = ((), (), s32[]{:S(2)}) async-start(), calls=%async_computation | async-start | bytes 13107200 | tf_op jit(solution)/shard_map/all_gather | solution.py:44
  9.4 17.9 %copy-start.2 = (bf16[64]{0:T(256)(128)(2,1)S(1)}, bf16[64]{0:T(256)(128)(2,1)}, u32[]{:S(2)}) copy-start(bf16[64]{0:T(256)(128)(2,1)} %param.7) | copy-start | bytes 388
  9.4 16.0 %collective-permute-start = (bf16[32,1,8192]{2,0,1:T(8,128)(2,1)S(1)}, bf16[32,1,8192]{2,0,1:T(8,128)(2,1)S(1)}, u32[]{:S(2)}, u32[]{:S(2)}) collective-permute-start(bf16[32,1,8192]{2,0,1:T(8,128)(2,1)S(1)} %slice.12), channel_id=1, source_target_pairs={{0,4},{4,8},{8,12},{12,16},{16,20},{20,24},{24,28},{1,5},{5,9},{9,... | collective-permute-start | bytes 1572872 | tf_op jit(solution)/shard_map/ppermute | solution.py:13
  27.2 175.0 %all-gather.5.cloned.1.call-start = ((), (), s32[]{:S(2)}) async-start(), calls=%async_computation.1 | async-start | bytes 3932160 | tf_op jit(solution)/shard_map/all_gather | solution.py:52
  135.2 9.0 %copy-start.1 = (bf16[27,64,128]{2,1,0:T(8,128)(2,1)S(1)}, bf16[27,64,128]{2,1,0:T(8,128)(2,1)}, u32[]{:S(2)}) copy-start(bf16[27,64,128]{2,1,0:T(8,128)(2,1)} %param.6) | copy-start | bytes 1327108
  135.2 9.0 %copy-start.4 = (pred[8,9]{0,1:T(8,128)(4,1)S(1)}, pred[8,9]{0,1:T(8,128)(4,1)}, u32[]{:S(2)}) copy-start(pred[8,9]{0,1:T(8,128)(4,1)} %constant.16) | copy-start | bytes 220
  159.8 12.7 %copy-start.3 = (bf16[64]{0:T(256)(128)(2,1)S(1)}, bf16[64]{0:T(256)(128)(2,1)}, u32[]{:S(2)}) copy-start(bf16[64]{0:T(256)(128)(2,1)} %param.9) | copy-start | bytes 388
  162.2 9.4 %collective-permute-start.1 = (bf16[64,1,2048]{2,0,1:T(8,128)(2,1)S(1)}, bf16[64,1,2048]{2,0,1:T(8,128)(2,1)S(1)}, u32[]{:S(2)}, u32[]{:S(2)}) collective-permute-start(bf16[64,1,2048]{2,0,1:T(8,128)(2,1)S(1)} %slice.15), channel_id=1, source_target_pairs={{0,4},{4,8},{8,12},{12,16},{16,20},{20,24},{24,28},{1,5},{5,9},{9,... | collective-permute-start | bytes 786440 | tf_op jit(solution)/shard_map/ppermute | solution.py:13
  211.0 2.5 %copy-start.5 = (pred[8,5]{0,1:T(8,128)(4,1)S(1)}, pred[8,5]{0,1:T(8,128)(4,1)}, u32[]{:S(2)}) copy-start(pred[8,5]{0,1:T(8,128)(4,1)} %constant.15) | copy-start | bytes 124
Sparse Core Ops, SparseCore 0:
  27.4 72.4 all-gather.2
  172.7 29.5 all-gather.4
where the time goes:
time: 225 us; the launch traced here: 224 us
  waiting for transfers between devices  119 us (53%)
  local copies, waits for them, and re-layouts  66.2 us (29%)
  between operations  13.6 us (6%)
  matrix products  12.7 us (6%)
  starting transfers between devices  8.31 us (4%)
  other arithmetic  3.7 us (2%)
    all_gather x1, waiting for transfers between devices, per_device(): lax.all_gather(extended, 'filter', axis=0, tiled=True)  72.5 us
    all_gather x1, waiting for transfers between devices, per_device(): lax.all_gather(extended_two, 'filter', axis=0, tiled=True)  29.7 us
    unnamed x15, local copies, waits for them, and re-layouts  21.3 us
    ppermute x2, waiting for transfers between devices, shifted(): return lax.ppermute(block, axis, route)  17.1 us
    conv_general_dilated x10, local copies, waits for them, and re-layouts, local_conv(): lax.conv_general_dilated(volume, kernel, (2, 2, 2), ((0, 0), (pad_rows, p...  17 us
    all_gather x1, local copies, waits for them, and re-layouts, per_device(): lax.all_gather(extended, 'filter', axis=0, tiled=True)  14.2 us
    conv_general_dilated x2, matrix products, local_conv(): lax.conv_general_dilated(volume, kernel, (2, 2, 2), ((0, 0), (pad_rows, p...  12.7 us
    ppermute x2, starting transfers between devices, shifted(): return lax.ppermute(block, axis, route)  8.26 us
  transfers between devices with their start and end apart: 4, of which 4 were waited for; matrix products, arithmetic and copies ran while one was open for 0% of the time, Pallas kernels for 0%

commit v1 on v0

--- a/solution.py
+++ b/solution.py
@@ -5,6 +5,18 @@
 
 ROWS = 64
 COLS = 128
+
+
+def doubled_up(array, axis, dim):
+    ways, here = (lax.axis_size(axis), lax.axis_index(axis))
+    grown, reach = (array, 1)
+    while reach < ways:
+        theirs = lax.ppermute(grown, axis, [(d, d ^ reach) for d in range(ways)])
+        mine_first = jnp.concatenate([grown, theirs], axis=dim)
+        theirs_first = jnp.concatenate([theirs, grown], axis=dim)
+        grown = jnp.where(here & reach == 0, mine_first, theirs_first)
+        reach = 2 * reach
+    return grown
 
 
 def shifted(block, axis, distance):
@@ -40,9 +52,7 @@
     extended = jnp.concatenate([beneath, volume_in], 1)
     zeros_first = jnp.zeros((outputs, slices // 2, ROWS // 2, COLS // 2), jnp.float32)
     weight_part = filters_a
-    summed = zeros_first + local_conv(
-        lax.all_gather(extended, "filter", axis=0, tiled=True), weight_part, 1, ROWS, COLS
-    )
+    summed = zeros_first + local_conv(doubled_up(extended, "filter", 0), weight_part, 1, ROWS, COLS)
     hidden = activate(summed, bias_a).reshape(outputs, slices // 2, ROWS // 2 * (COLS // 2))
     beneath_two = shifted(hidden[:, -1:], "spatial", 1)
     extended_two = jnp.concatenate([beneath_two, hidden], 1)

time: 225 us -> 278 us (1.24)
  waiting for transfers between devices: 119 us -> 159 us
  other arithmetic: 3.7 us -> 18.3 us
  local copies, waits for them, and re-layouts: 66.2 us -> 63.1 us
    ppermute x0 -> x2, waiting for transfers between devices: none -> 111 us  [doubled_up(): theirs = lax.ppermute(grown, axis, [(d, d ^ reach) for d in range(ways)])]
    all_gather x1 -> x0, waiting for transfers between devices: 72.5 us -> none  [per_device(): lax.all_gather(extended, 'filter', axis=0, tiled=True)]
    all_gather x1 -> x0, local copies, waits for them, and re-layouts: 14.2 us -> none  [per_device(): lax.all_gather(extended, 'filter', axis=0, tiled=True)]
    select_n x0 -> x2, other arithmetic: none -> 11.4 us  [doubled_up(): grown = jnp.where(here & reach == 0, mine_first, theirs_first)]
    unnamed x15 -> x21, local copies, waits for them, and re-layouts: 21.3 us -> 28.2 us
    reshape x2 -> x1, local copies, waits for them, and re-layouts: 6.84 us -> 0.42 us  [local_conv(): volume = block.reshape(1, channels, slices, row_count, col_count)]
    select_n x0 -> x1, local copies, waits for them, and re-layouts: none -> 6.43 us  [doubled_up(): grown = jnp.where(here & reach == 0, mine_first, theirs_first)]
    concatenate x1, other arithmetic: 1.78 us -> 4.89 us  [doubled_up(): mine_first = jnp.concatenate([grown, theirs], axis=dim)]
  transfers between devices with their start and end apart: 4 -> 5, of which waited for: 4 -> 5; matrix products, arithmetic and copies ran while one was open for 0% -> 3% of each run, Pallas kernels for 0% -> 0%
where the time goes in v1:
time: 278 us; the launch traced here: 277 us
  waiting for transfers between devices  159 us (57%)
  local copies, waits for them, and re-layouts  63.1 us (23%)
  other arithmetic  18.3 us (7%)
  between operations  13.7 us (5%)
  matrix products  12.7 us (5%)
  starting transfers between devices  10.9 us (4%)
    ppermute x2, waiting for transfers between devices, doubled_up(): theirs = lax.ppermute(grown, axis, [(d, d ^ reach) for d in range(ways)])  111 us
    all_gather x1, waiting for transfers between devices, per_device(): lax.all_gather(extended_two, 'filter', axis=0, tiled=True)  31.8 us
    unnamed x21, local copies, waits for them, and re-layouts  28.2 us
    conv_general_dilated x10, local copies, waits for them, and re-layouts, local_conv(): lax.conv_general_dilated(volume, kernel, (2, 2, 2), ((0, 0), (pad_rows, p...  17 us
    ppermute x2, waiting for transfers between devices, shifted(): return lax.ppermute(block, axis, route)  16.1 us
    conv_general_dilated x2, matrix products, local_conv(): lax.conv_general_dilated(volume, kernel, (2, 2, 2), ((0, 0), (pad_rows, p...  12.7 us
    select_n x2, other arithmetic, doubled_up(): grown = jnp.where(here & reach == 0, mine_first, theirs_first)  11.4 us
    ppermute x2, starting transfers between devices, shifted(): return lax.ppermute(block, axis, route)  9.28 us
  transfers between devices with their start and end apart: 5, of which 5 were waited for; matrix products, arithmetic and copies ran while one was open for 3% of the time, Pallas kernels for 0%

profile of v1, /device:TPU:0, one launch (start us, length us, event | category | flops | bytes accessed | tf_op | source)
XLA Modules:
  0.0 277.3 jit_solution(8228020014091951424)
XLA Ops:
  6.5 0.0 copy-start
  6.5 0.0 all-gather.2.cloned.1.call-start
  6.5 0.0 copy-start.1
  6.5 3.0 %slice.12 = bf16[32,1,8192]{2,1,0:T(2,128)(2,1)S(1)} slice(bf16[32,4,8192]{2,1,0:T(4,128)(2,1)} %param.5), slice={[0:32], [3:4], [0:8192]} | slice | bytes 1048576 | tf_op jit(solution)/shard_map/slice | solution.py:51
  9.6 0.6 copy.67
  10.1 4.9 %collective-permute-start = (bf16[32,1,8192]{2,0,1:T(8,128)(2,1)S(1)}, bf16[32,1,8192]{2,0,1:T(8,128)(2,1)S(1)}, u32[]{:S(2)}, u32[]{:S(2)}) collective-permute-start(bf16[32,1,8192]{2,0,1:T(8,128)(2,1)S(1)} %copy.67), channel_id=1, source_target_pairs={{0,4},{4,8},{8,12},{12,16},{16,20},{20,24},{24,28},{1,5},{5,9},{9,... | collective-permute-start | bytes 1572872 | tf_op jit(solution)/shard_map/ppermute | solution.py:25
  15.0 11.1 %collective-permute-done = bf16[32,1,8192]{2,0,1:T(8,128)(2,1)S(1)} collective-permute-done((bf16[32,1,8192]{2,0,1:T(8,128)(2,1)S(1)}, bf16[32,1,8192]{2,0,1:T(8,128)(2,1)S(1)}, u32[]{:S(2)}, u32[]{:S(2)}) %collective-permute-start) | collective-permute-done | bytes 524320 | tf_op jit(solution)/shard_map/ppermute | solution.py:25
  26.2 0.0 copy-done.1
  26.2 1.2 constant_dynamic-update-slice_fusion
  27.4 0.1 collective-permute-start.1
  27.5 0.0 copy-start.3
  27.5 5.0 %collective-permute-done.1 = bf16[32,5,8192]{2,0,1:T(8,128)(2,1)} collective-permute-done((bf16[32,5,8192]{2,0,1:T(8,128)(2,1)S(1)}, bf16[32,5,8192]{2,0,1:T(8,128)(2,1)}, u32[]{:S(2)}, u32[]{:S(2)}) %collective-permute-start.1) | collective-permute-done | bytes 2621472 | tf_op jit(solution)/shard_map/ppermute | solution.py:14
  32.5 6.4 %maximum_select_fusion.2 = bf16[64,5,8192]{2,0,1:T(8,128)(2,1)} fusion(bf16[32,5,8192]{2,0,1:T(8,128)(2,1)} %collective-permute-done.1, bf16[32,5,8192]{2,0,1:T(8,128)(2,1)S(1)} %constant_dynamic-update-slice_fusion, pred[]{:T(512)S(6)} %eq.7), kind=kLoop, calls=%fused_computation.12 | loop fusion | flops 23592960 | bytes 10485761 | tf_op jit(solution)/shard_map/jit(_where)/select_n | solution.py:17
  38.9 1.5 collective-permute-start.2
  40.4 0.0 copy-done.3
  40.4 0.7 copy.63
  41.2 2.5 copy.64
  43.6 4.9 %fusion.8 = bf16[1,64,5,64,128]{4,3,1,2,0:T(8,128)(2,1)S(1)} fusion(bf16[32,5,64,128]{3,2,0,1:T(8,128)(2,1)S(1)} %bitcast.57, bf16[32,5,64,128]{3,2,0,1:T(8,128)(2,1)S(1)} %bitcast.56, pred[]{:T(512)S(6)} %eq.7), kind=kLoop, calls=%fused_computation.11 | loop fusion | flops 7864320 | bytes 10485761 | tf_op jit(solution)/shard_map/concatenate | solution.py:15
  48.5 105.8 %collective-permute-done.2 = bf16[64,5,8192]{2,0,1:T(8,128)(2,1)} collective-permute-done((bf16[64,5,8192]{2,0,1:T(8,128)(2,1)}, bf16[64,5,8192]{2,0,1:T(8,128)(2,1)}, u32[]{:S(2)}, u32[]{:S(2)}) %collective-permute-start.2) | collective-permute-done | bytes 5242912 | tf_op jit(solution)/shard_map/ppermute | solution.py:14
  154.3 4.0 %copy.65 = bf16[40,8,64,128]{3,2,1,0:T(8,128)(2,1)S(1)} copy(bf16[40,8,64,128]{3,1,2,0:T(8,128)(2,1)} %bitcast.28) | data formatting | bytes 10485760
  158.3 5.0 %fusion.5 = bf16[128,5,64,1,128]{4,2,0,1,3:T(8,128)(2,1)} fusion(bf16[1,64,5,64,128]{4,3,1,2,0:T(8,128)(2,1)S(1)} %bitcast.52, bf16[1,64,5,64,128]{4,3,1,2,0:T(8,128)(2,1)S(1)} %fusion.8, pred[]{:T(512)S(6)} %eq.6), kind=kLoop, calls=%fused_computation.6 | loop fusion | flops 15728640 | bytes 20971520 | tf_op jit(solution)/shard_map/jit(_where)/select_n | solution.py:17
  163.3 16.8 %copy.61 = bf16[128,5,64,1,128]{0,2,4,1,3:T(8,128)(2,1)} copy(bf16[128,5,64,1,128]{4,2,0,1,3:T(8,128)(2,1)} %fusion.5) | data formatting | bytes 20971520
  180.1 6.4 %pad.clone = bf16[128,5,64,1,144]{0,2,4,1,3:T(8,128)(2,1)S(1)} pad(bf16[128,5,64,1,128]{0,2,4,1,3:T(8,128)(2,1)} %copy.61, bf16[]{:T(256)} %constant.5), padding=0_0x0_0x0_0x0_0x1_15 | pad | bytes 22282242 | tf_op jit(solution)/shard_map/jit(_where)/select_n | solution.py:17
  186.5 0.0 copy-start.2
  186.5 0.0 copy-start.5
  186.5 8.6 %copy.51 = bf16[128,5,64,1,8,18]{0,4,5,2,1,3:T(8,128)(2,1)S(1)} copy(bf16[128,5,64,1,8,18]{0,2,5,4,1,3:T(8,128)(2,1)S(1)} %bitcast.51) | data formatting | bytes 23592960 | tf_op jit(solution)/shard_map/conv_general_dilated | solution.py:33
  195.2 0.3 slice.13
  195.5 0.0 copy-done.2
  195.5 0.0 copy-done.5
  195.5 10.2 %fusion.14 = f32[2,32,8,9,64]{4,2,3,1,0:T(8,128)} fusion(bf16[3,3,3,64,128]{4,3,2,1,0:T(8,128)(2,1)S(1)} %bitcast.61, bf16[128,5,64,1,7,2]{0,4,5,2,1,3:T(8,128)(2,1)S(1)} %slice.13, bf16[128,5,64,1,8,18]{0,4,5,2,1,3:T(8,128)(2,1)S(1)} %copy.51, pred[8,9]{0,1:T(8,128)(4,1)S(1)} %copy-done.5), kind=kOutput, calls=%fused_computation.19 | convolution fusion | flops 2056814592 | bytes 14565448 | tf_op jit(solution)/shard_map/conv_general_dilated | solution.py:33
  205.8 2.1 copy.52
  207.9 0.2 slice_bitcast_fusion
  208.1 0.0 copy-start.4
  208.1 3.1 %copy.53 = f32[1,64,2,32,64]{4,3,1,2,0:T(8,128)} copy(f32[1,64,2,32,64]{1,3,4,2,0:T(8,128)S(1)} %slice_bitcast_fusion) | data formatting | bytes 2097152 | tf_op jit(solution)/shard_map/conv_general_dilated | solution.py:33
  211.1 2.1 squeeze.6
  213.2 0.2 fusion.20
  213.5 4.4 %collective-permute-start.3 = (bf16[64,1,2048]{2,0,1:T(8,128)(2,1)S(1)}, bf16[64,1,2048]{2,0,1:T(8,128)(2,1)S(1)}, u32[]{:S(2)}, u32[]{:S(2)}) collective-permute-start(bf16[64,1,2048]{2,0,1:T(8,128)(2,1)S(1)} %slice.15), channel_id=1, source_target_pairs={{0,4},{4,8},{8,12},{12,16},{16,20},{20,24},{24,28},{1,5},{5,9},{9,... | collective-permute-start | bytes 786440 | tf_op jit(solution)/shard_map/ppermute | solution.py:25
  217.9 5.0 %collective-permute-done.3 = bf16[64,1,2048]{2,0,1:T(8,128)(2,1)S(1)} collective-permute-done((bf16[64,1,2048]{2,0,1:T(8,128)(2,1)S(1)}, bf16[64,1,2048]{2,0,1:T(8,128)(2,1)S(1)}, u32[]{:S(2)}, u32[]{:S(2)}) %collective-permute-start.3) | collective-permute-done | bytes 262176 | tf_op jit(solution)/shard_map/ppermute | solution.py:25
  222.9 1.0 pad_maximum_fusion
  223.9 0.0 all-gather.2.cloned.1.call-update
  223.9 0.0 copy-done.4
  223.9 31.8 %all-gather.2.cloned.1.call-done = bf16[256,3,2048]{2,0,1:T(8,128)(2,1)} async-done(((bf16[64,3,2048]{2,0,1:T(8,128)(2,1)}), bf16[256,3,2048]{2,0,1:T(8,128)(2,1)}) %all-gather.2.cloned.1.call-update) | async-done | bytes 3145744 | tf_op jit(solution)/shard_map/all_gather | solution.py:62
  255.7 4.6 %copy.54 = bf16[256,3,2048]{0,2,1:T(8,128)(2,1)} copy(bf16[256,3,2048]{2,0,1:T(8,128)(2,1)} %all-gather.2.cloned.1.call-done) | data formatting | bytes 6291456 | tf_op jit(solution)/shard_map/all_gather | solution.py:62
  260.3 3.7 %copy.62 = bf16[256,3,32,1,64]{0,2,4,1,3:T(8,128)(2,1)S(1)} copy(bf16[256,3,32,1,64]{0,4,2,1,3:T(8,128)(2,1)} %bitcast.55) | data formatting | bytes 6291456
  264.0 0.4 pad.2.clone
  264.4 0.0 copy-start.6
  264.5 2.3 copy.57
  266.7 0.2 slice.16
  266.9 0.0 copy-done
  266.9 0.0 copy-done.6
  267.0 2.5 fusion.17
  269.4 0.1 copy.58
  269.5 0.1 copy.59
  269.6 0.1 copy.60
  269.7 0.7 fusion.21
  (5 shorter events, 0.1 us)
Async XLA Ops:
  6.5 260.4 %copy-start = (bf16[27,64,256]{2,1,0:T(8,128)(2,1)S(1)}, bf16[27,64,256]{2,1,0:T(8,128)(2,1)}, u32[]{:S(2)}) copy-start(bf16[27,64,256]{2,1,0:T(8,128)(2,1)} %param.8) | copy-start | bytes 2654212
  6.5 249.2 %all-gather.2.cloned.1.call-start = ((), (), s32[]{:S(2)}) async-start(), calls=%async_computation | async-start | bytes 3932160 | tf_op jit(solution)/shard_map/all_gather | solution.py:62
  6.5 19.7 %copy-start.1 = (bf16[32,4,8192]{2,1,0:T(4,128)(2,1)S(1)}, bf16[32,4,8192]{2,1,0:T(4,128)(2,1)}, u32[]{:S(2)}) copy-start(bf16[32,4,8192]{2,1,0:T(4,128)(2,1)} %param.5) | copy-start | bytes 6291460
  10.1 16.0 %collective-permute-start = (bf16[32,1,8192]{2,0,1:T(8,128)(2,1)S(1)}, bf16[32,1,8192]{2,0,1:T(8,128)(2,1)S(1)}, u32[]{:S(2)}, u32[]{:S(2)}) collective-permute-start(bf16[32,1,8192]{2,0,1:T(8,128)(2,1)S(1)} %copy.67), channel_id=1, source_target_pairs={{0,4},{4,8},{8,12},{12,16},{16,20},{20,24},{24,28},{1,5},{5,9},{9,... | collective-permute-start | bytes 1572872 | tf_op jit(solution)/shard_map/ppermute | solution.py:25
  27.4 5.1 %collective-permute-start.1 = (bf16[32,5,8192]{2,0,1:T(8,128)(2,1)S(1)}, bf16[32,5,8192]{2,0,1:T(8,128)(2,1)}, u32[]{:S(2)}, u32[]{:S(2)}) collective-permute-start(bf16[32,5,8192]{2,0,1:T(8,128)(2,1)S(1)} %constant_dynamic-update-slice_fusion), channel_id=1, source_target_pairs={{0,1},{1,0},{2,3},{3,2},{4,5},{5,4},{6,7},{7,6},{8,9},{9,8},{10,11... | collective-permute-start | bytes 7864328 | tf_op jit(solution)/shard_map/ppermute | solution.py:14
  27.5 13.0 %copy-start.3 = (bf16[64]{0:T(256)(128)(2,1)S(1)}, bf16[64]{0:T(256)(128)(2,1)}, u32[]{:S(2)}) copy-start(bf16[64]{0:T(256)(128)(2,1)} %param.7) | copy-start | bytes 388
  38.9 115.4 %collective-permute-start.2 = (bf16[64,5,8192]{2,0,1:T(8,128)(2,1)}, bf16[64,5,8192]{2,0,1:T(8,128)(2,1)}, u32[]{:S(2)}, u32[]{:S(2)}) collective-permute-start(bf16[64,5,8192]{2,0,1:T(8,128)(2,1)} %maximum_select_fusion.2), channel_id=1, source_target_pairs={{0,2},{1,3},{2,0},{3,1},{4,6},{5,7},{6,4},{7,5},{8,10},{9,11},{10,... | collective-permute-start | bytes 15728648 | tf_op jit(solution)/shard_map/ppermute | solution.py:14
  186.5 9.0 %copy-start.2 = (bf16[27,64,128]{2,1,0:T(8,128)(2,1)S(1)}, bf16[27,64,128]{2,1,0:T(8,128)(2,1)}, u32[]{:S(2)}) copy-start(bf16[27,64,128]{2,1,0:T(8,128)(2,1)} %param.6) | copy-start | bytes 1327108
  186.5 9.0 %copy-start.5 = (pred[8,9]{0,1:T(8,128)(4,1)S(1)}, pred[8,9]{0,1:T(8,128)(4,1)}, u32[]{:S(2)}) copy-start(pred[8,9]{0,1:T(8,128)(4,1)} %constant.26) | copy-start | bytes 220
  208.1 15.8 %copy-start.4 = (bf16[64]{0:T(256)(128)(2,1)S(1)}, bf16[64]{0:T(256)(128)(2,1)}, u32[]{:S(2)}) copy-start(bf16[64]{0:T(256)(128)(2,1)} %param.9) | copy-start | bytes 388
  213.5 9.4 %collective-permute-start.3 = (bf16[64,1,2048]{2,0,1:T(8,128)(2,1)S(1)}, bf16[64,1,2048]{2,0,1:T(8,128)(2,1)S(1)}, u32[]{:S(2)}, u32[]{:S(2)}) collective-permute-start(bf16[64,1,2048]{2,0,1:T(8,128)(2,1)S(1)} %slice.15), channel_id=1, source_target_pairs={{0,4},{4,8},{8,12},{12,16},{16,20},{20,24},{24,28},{1,5},{5,9},{9,... | collective-permute-start | bytes 786440 | tf_op jit(solution)/shard_map/ppermute | solution.py:25
  264.4 2.5 copy-start.6
Sparse Core Ops, SparseCore 0:
  224.0 31.6 all-gather.1
